TPU v7x, 256 devices: a whole 4x4x8 slice. The times are simulated.
256 devices in a mesh: row: 32 (over z, y_hi, core), off: 8 (over x, y_lo).
Axes of the slice: x: 4, y: 4 (y_hi: 2, y_lo: 2; y = y_hi * 2 + y_lo), z: 8, core: 2. Of those that a mesh axis runs over, the one named last changes fastest.
Arguments:
- vectors: float32 [32768, 128], P(('row', 'off')), may hold values from -6 to 6
- blocks: float32 [32, 8, 48, 128, 128], P('row', 'off'), may hold values from -0.0546875 to 0.0546875
- lists: int32 [32, 8, 2, 48], P('row', 'off'), may hold values from 0 to 7, as said below
Outputs:
- filtered: float32 [32768, 128], P(('row', 'off'))
Inputs may be any that keep to these rules, and one draw needn't show every extreme that they name: `lists`: within each tile the 48 listed blocks are distinct positions of its 8 x 8 grid of blocks.
All inputs are finite; a program needn't handle non-finite values.
Results may differ from a plain program's by a relative error of at most 0.00011.
Values sent between devices are 32-bit elements; how exact they have to be, the bound alone decides.
A program may use at most 64 MiB of HBM per device.

v0:
```python
import jax
import jax.numpy as jnp
from jax import lax
from jax.sharding import PartitionSpec as P

DEGREE = 4
first_scale = 0.4
later_scale = 0.8


def passed_along(block, axis, distance):
    devices = range(lax.axis_size(axis))
    route = [((i - distance) % len(devices), i) for i in devices]
    return lax.ppermute(block, axis, route)


def per_device(vectors, blocks, lists):
    n_offsets = lax.axis_size("off")
    offset_index = lax.axis_index("off")
    piece_rows = vectors.shape[0]
    tile_rows = piece_rows * n_offsets
    width = vectors.shape[1]
    block_size = blocks.shape[-1]
    per_side = tile_rows // block_size
    stored = blocks[0, 0]
    row_list = lists[0, 0, 0]
    col_list = lists[0, 0, 1]
    positions = jnp.arange(per_side, dtype=jnp.int32)
    row_onehot = (row_list[:, None] == positions[None, :]).astype(jnp.float32)
    col_onehot = (col_list[:, None] == positions[None, :]).astype(jnp.float32)
    bit_count = (n_offsets - 1).bit_length()

    def pull(field):
        for bit_number in range(bit_count):
            moved = passed_along(field, "row", -(1 << bit_number))
            field = jnp.where(offset_index // (1 << bit_number) % 2 == 1, moved, field)
        return field

    def push(field):
        for bit_number in range(bit_count):
            moved = passed_along(field, "row", 1 << bit_number)
            field = jnp.where(offset_index // (1 << bit_number) % 2 == 1, moved, field)
        return field

    def apply_tiles(gathered):
        own = gathered.reshape(per_side, block_size, width)
        transposed = jnp.einsum(
            "kab,kav->kbv", stored, own[row_list], precision=lax.Precision.HIGHEST
        )
        back_terms = jnp.einsum(
            "kt,kbv->tbv", col_onehot, transposed, precision=lax.Precision.HIGHEST
        )
        returned = push(back_terms.reshape(tile_rows, width))
        far_field = pull(gathered).reshape(per_side, block_size, width)
        direct = jnp.einsum(
            "kab,kbv->kav", stored, far_field[col_list], precision=lax.Precision.HIGHEST
        )
        ahead = jnp.einsum("kt,kav->tav", row_onehot, direct, precision=lax.Precision.HIGHEST)
        return ahead.reshape(tile_rows, width) + returned

    def spread(piece):
        return lax.all_gather(piece, "off", axis=0, tiled=True)

    def fold(terms):
        return lax.psum_scatter(terms, "off", scatter_dimension=0, tiled=True)

    previous = vectors
    current = first_scale * fold(apply_tiles(spread(vectors)))
    for degree in range(1, DEGREE):
        following = later_scale * fold(apply_tiles(spread(current))) - previous
        previous, current = (current, following)
    return current


def solution(mesh):
    in_specs = (
        P(("row", "off"), None),
        P("row", "off", None, None, None),
        P("row", "off", None, None),
    )
    out_specs = P(("row", "off"), None)
    return jax.shard_map(
        per_device, mesh=mesh, in_specs=in_specs, out_specs=out_specs, check_vma=False
    )
```

profile of v0, /device:TPU:32, one launch (start us, length us, event | category | flops | bytes accessed | tf_op | source)
XLA Modules:
  0.0 610.8 jit_solution(9065694514423480050)
XLA Ops:
  6.5 31.6 %all_gather.12 = f32[1024,128]{1,0:T(8,128)} all-gather(f32[128,128]{1,0:T(8,128)} %param.3), channel_id=1, replica_groups=mesh['row'=32,'off'=8] {'off'}, dimensions={0}, use_global_device_ids=true | all-gather | bytes 589824 | tf_op jit(solution)/shard_map/all_gather | solution.py:62
  38.9 3.5 gather_fusion.1
  42.4 7.9 %fusion.28 = f32[48,128,128]{2,1,0:T(8,128)} fusion(f32[48,128,128]{2,1,0:T(8,128)} %gather_fusion.1, f32[1,1,48,128,128]{4,3,2,1,0:T(8,128)S(1)} %copy-done), kind=kOutput, calls=%fused_computation.36 | convolution fusion | flops 1207959552 | bytes 9437184 | tf_op jit(solution)/shard_map/kab,kav->kbv/dot_general | solution.py:47
  50.2 3.6 copy.13
  53.8 3.0 fusion.12
  62.9 6.2 %collective-permute-done.3 = f32[1024,128]{1,0:T(8,128)} collective-permute-done((f32[1024,128]{1,0:T(8,128)}, f32[1024,128]{1,0:T(8,128)}, u32[]{:S(2)}, u32[]{:S(2)}) %collective-permute-start.3) | collective-permute-done | bytes 524320 | tf_op jit(solution)/shard_map/ppermute | solution.py:14
  71.1 13.5 %collective-permute-start.4 = (f32[1024,128]{1,0:T(8,128)}, f32[1024,128]{1,0:T(8,128)}, u32[]{:S(2)}, u32[]{:S(2)}) collective-permute-start(f32[1024,128]{1,0:T(8,128)} %broadcast_select_fusion.6), channel_id=1, source_target_pairs={{240,0},{248,8},{0,16},{8,24},{16,32},{24,40},{32,48},{40,56},{48,... | collective-permute-start | bytes 1572872 | tf_op jit(solution)/shard_map/ppermute | solution.py:14
  86.6 10.5 %collective-permute-done.4 = f32[1024,128]{1,0:T(8,128)} collective-permute-done((f32[1024,128]{1,0:T(8,128)}, f32[1024,128]{1,0:T(8,128)}, u32[]{:S(2)}, u32[]{:S(2)}) %collective-permute-start.4) | collective-permute-done | bytes 524320 | tf_op jit(solution)/shard_map/ppermute | solution.py:14
  103.1 3.5 gather_fusion
  106.5 7.9 %fusion.30 = f32[48,128,128]{2,1,0:T(8,128)} fusion(f32[48,128,128]{2,1,0:T(8,128)} %gather_fusion, f32[1,1,48,128,128]{4,3,2,1,0:T(8,128)S(1)} %copy-done), kind=kOutput, calls=%fused_computation.38 | convolution fusion | flops 1207959552 | bytes 9437184 | tf_op jit(solution)/shard_map/kab,kbv->kav/dot_general | solution.py:55
  114.4 3.6 copy.12
  118.0 3.0 fusion.14
  123.2 40.0 %reduce-scatter.5.cloned.1.call-done = f32[128,128]{1,0:T(8,128)} async-done(((f32[1024,128]{1,0:T(8,128)}), f32[128,128]{1,0:T(8,128)}) %reduce-scatter.5.cloned.1.call-update) | async-done | bytes 65552 | tf_op jit(solution)/shard_map/reduce_scatter | solution.py:65
  164.0 31.1 %all_gather.13 = f32[1024,128]{1,0:T(8,128)} all-gather(f32[128,128]{1,0:T(8,128)S(1)} %broadcast_multiply_fusion), channel_id=1, replica_groups=mesh['row'=32,'off'=8] {'off'}, dimensions={0}, use_global_device_ids=true | all-gather | bytes 589824 | tf_op jit(solution)/shard_map/all_gather | solution.py:62
  195.1 3.5 gather_fusion.3
  198.6 7.9 %fusion.24 = f32[48,128,128]{2,1,0:T(8,128)} fusion(f32[48,128,128]{2,1,0:T(8,128)} %gather_fusion.3, f32[1,1,48,128,128]{4,3,2,1,0:T(8,128)S(1)} %copy-done), kind=kOutput, calls=%fused_computation.32 | convolution fusion | flops 1207959552 | bytes 9437184 | tf_op jit(solution)/shard_map/kab,kav->kbv/dot_general | solution.py:47
  206.5 3.5 copy.15
  217.6 6.7 %collective-permute-done.9 = f32[1024,128]{1,0:T(8,128)S(1)} collective-permute-done((f32[1024,128]{1,0:T(8,128)S(1)}, f32[1024,128]{1,0:T(8,128)S(1)}, u32[]{:S(2)}, u32[]{:S(2)}) %collective-permute-start.9) | collective-permute-done | bytes 524320 | tf_op jit(solution)/shard_map/ppermute | solution.py:14
  224.4 12.9 %collective-permute-start.10 = (f32[1024,128]{1,0:T(8,128)S(1)}, f32[1024,128]{1,0:T(8,128)S(1)}, u32[]{:S(2)}, u32[]{:S(2)}) collective-permute-start(f32[1024,128]{1,0:T(8,128)S(1)} %broadcast_select_fusion.4), channel_id=1, source_target_pairs={{240,0},{248,8},{0,16},{8,24},{16,32},{24,40},{32,48},{40,56},{48,... | collective-permute-start | bytes 1572872 | tf_op jit(solution)/shard_map/ppermute | solution.py:14
  237.7 11.9 %collective-permute-done.10 = f32[1024,128]{1,0:T(8,128)S(1)} collective-permute-done((f32[1024,128]{1,0:T(8,128)S(1)}, f32[1024,128]{1,0:T(8,128)S(1)}, u32[]{:S(2)}, u32[]{:S(2)}) %collective-permute-start.10) | collective-permute-done | bytes 524320 | tf_op jit(solution)/shard_map/ppermute | solution.py:14
  253.0 3.4 gather_fusion.2
  256.4 7.9 %fusion.26 = f32[48,128,128]{2,1,0:T(8,128)} fusion(f32[48,128,128]{2,1,0:T(8,128)} %gather_fusion.2, f32[1,1,48,128,128]{4,3,2,1,0:T(8,128)S(1)} %copy-done), kind=kOutput, calls=%fused_computation.34 | convolution fusion | flops 1207959552 | bytes 9437184 | tf_op jit(solution)/shard_map/kab,kbv->kav/dot_general | solution.py:55
  264.3 3.6 copy.14
  267.9 3.0 fusion.10
  273.1 36.3 %reduce-scatter.7.cloned.1.call-done = f32[128,128]{1,0:T(8,128)} async-done(((f32[1024,128]{1,0:T(8,128)}), f32[128,128]{1,0:T(8,128)}) %reduce-scatter.7.cloned.1.call-update) | async-done | bytes 65552 | tf_op jit(solution)/shard_map/reduce_scatter | solution.py:65
  310.2 31.1 %all_gather.14 = f32[1024,128]{1,0:T(8,128)} all-gather(f32[128,128]{1,0:T(8,128)S(1)} %multiply_subtract_fusion.2), channel_id=1, replica_groups=mesh['row'=32,'off'=8] {'off'}, dimensions={0}, use_global_device_ids=true | all-gather | bytes 589824 | tf_op jit(solution)/shard_map/all_gather | solution.py:62
  341.5 3.5 gather_fusion.5
  345.0 7.9 %fusion.20 = f32[48,128,128]{2,1,0:T(8,128)} fusion(f32[48,128,128]{2,1,0:T(8,128)} %gather_fusion.5, f32[1,1,48,128,128]{4,3,2,1,0:T(8,128)S(1)} %copy-done), kind=kOutput, calls=%fused_computation.28 | convolution fusion | flops 1207959552 | bytes 9437184 | tf_op jit(solution)/shard_map/kab,kav->kbv/dot_general | solution.py:47
  352.8 3.5 copy.17
  363.6 7.0 %collective-permute-done.15 = f32[1024,128]{1,0:T(8,128)S(1)} collective-permute-done((f32[1024,128]{1,0:T(8,128)S(1)}, f32[1024,128]{1,0:T(8,128)S(1)}, u32[]{:S(2)}, u32[]{:S(2)}) %collective-permute-start.15) | collective-permute-done | bytes 524320 | tf_op jit(solution)/shard_map/ppermute | solution.py:14
  370.8 12.9 %collective-permute-start.16 = (f32[1024,128]{1,0:T(8,128)S(1)}, f32[1024,128]{1,0:T(8,128)S(1)}, u32[]{:S(2)}, u32[]{:S(2)}) collective-permute-start(f32[1024,128]{1,0:T(8,128)S(1)} %broadcast_select_fusion.2), channel_id=1, source_target_pairs={{240,0},{248,8},{0,16},{8,24},{16,32},{24,40},{32,48},{40,56},{48,... | collective-permute-start | bytes 1572872 | tf_op jit(solution)/shard_map/ppermute | solution.py:14
  384.2 11.9 %collective-permute-done.16 = f32[1024,128]{1,0:T(8,128)S(1)} collective-permute-done((f32[1024,128]{1,0:T(8,128)S(1)}, f32[1024,128]{1,0:T(8,128)S(1)}, u32[]{:S(2)}, u32[]{:S(2)}) %collective-permute-start.16) | collective-permute-done | bytes 524320 | tf_op jit(solution)/shard_map/ppermute | solution.py:14
  399.8 3.4 gather_fusion.4
  403.2 7.9 %fusion.22 = f32[48,128,128]{2,1,0:T(8,128)} fusion(f32[48,128,128]{2,1,0:T(8,128)} %gather_fusion.4, f32[1,1,48,128,128]{4,3,2,1,0:T(8,128)S(1)} %copy-done), kind=kOutput, calls=%fused_computation.30 | convolution fusion | flops 1207959552 | bytes 9437184 | tf_op jit(solution)/shard_map/kab,kbv->kav/dot_general | solution.py:55
  411.1 3.6 copy.16
  414.6 3.0 fusion.6
  419.8 36.2 %reduce-scatter.9.cloned.1.call-done = f32[128,128]{1,0:T(8,128)} async-done(((f32[1024,128]{1,0:T(8,128)}), f32[128,128]{1,0:T(8,128)}) %reduce-scatter.9.cloned.1.call-update) | async-done | bytes 65552 | tf_op jit(solution)/shard_map/reduce_scatter | solution.py:65
  456.9 31.3 %all_gather.15 = f32[1024,128]{1,0:T(8,128)} all-gather(f32[128,128]{1,0:T(8,128)S(1)} %multiply_subtract_fusion.1), channel_id=1, replica_groups=mesh['row'=32,'off'=8] {'off'}, dimensions={0}, use_global_device_ids=true | all-gather | bytes 589824 | tf_op jit(solution)/shard_map/all_gather | solution.py:62
  488.2 3.5 gather_fusion.7
  491.7 7.9 %fusion.16 = f32[48,128,128]{2,1,0:T(8,128)} fusion(f32[48,128,128]{2,1,0:T(8,128)} %gather_fusion.7, f32[1,1,48,128,128]{4,3,2,1,0:T(8,128)S(1)} %copy-done), kind=kOutput, calls=%fused_computation.24 | convolution fusion | flops 1207959552 | bytes 9437184 | tf_op jit(solution)/shard_map/kab,kav->kbv/dot_general | solution.py:47
  499.6 3.6 copy.19
  510.5 7.0 %collective-permute-done.21 = f32[1024,128]{1,0:T(8,128)S(1)} collective-permute-done((f32[1024,128]{1,0:T(8,128)S(1)}, f32[1024,128]{1,0:T(8,128)S(1)}, u32[]{:S(2)}, u32[]{:S(2)}) %collective-permute-start.21) | collective-permute-done | bytes 524320 | tf_op jit(solution)/shard_map/ppermute | solution.py:14
  517.5 12.6 %collective-permute-start.22 = (f32[1024,128]{1,0:T(8,128)S(1)}, f32[1024,128]{1,0:T(8,128)S(1)}, u32[]{:S(2)}, u32[]{:S(2)}) collective-permute-start(f32[1024,128]{1,0:T(8,128)S(1)} %broadcast_select_fusion), channel_id=1, source_target_pairs={{240,0},{248,8},{0,16},{8,24},{16,32},{24,40},{32,48},{40,56},{48,... | collective-permute-start | bytes 1572872 | tf_op jit(solution)/shard_map/ppermute | solution.py:14
  530.7 11.8 %collective-permute-done.22 = f32[1024,128]{1,0:T(8,128)S(1)} collective-permute-done((f32[1024,128]{1,0:T(8,128)S(1)}, f32[1024,128]{1,0:T(8,128)S(1)}, u32[]{:S(2)}, u32[]{:S(2)}) %collective-permute-start.22) | collective-permute-done | bytes 524320 | tf_op jit(solution)/shard_map/ppermute | solution.py:14
  545.8 3.4 gather_fusion.6
  549.2 7.9 %fusion.18 = f32[48,128,128]{2,1,0:T(8,128)} fusion(f32[48,128,128]{2,1,0:T(8,128)} %gather_fusion.6, f32[1,1,48,128,128]{4,3,2,1,0:T(8,128)S(1)} %copy-done), kind=kOutput, calls=%fused_computation.26 | convolution fusion | flops 1207959552 | bytes 9437184 | tf_op jit(solution)/shard_map/kab,kbv->kav/dot_general | solution.py:55
  557.1 3.6 copy.18
  565.9 36.5 %reduce-scatter.11.cloned.1.call-done = f32[128,128]{1,0:T(8,128)} async-done(((f32[1024,128]{1,0:T(8,128)}), f32[128,128]{1,0:T(8,128)}) %reduce-scatter.11.cloned.1.call-update) | async-done | bytes 65552 | tf_op jit(solution)/shard_map/reduce_scatter | solution.py:65
  (96 shorter events, 66.7 us)
Async XLA Ops:
  6.5 35.8 %copy-start = (f32[1,1,48,128,128]{4,3,2,1,0:T(8,128)S(1)}, f32[1,1,48,128,128]{4,3,2,1,0:T(8,128)}, u32[]{:S(2)}) copy-start(f32[1,1,48,128,128]{4,3,2,1,0:T(8,128)} %param.4) | copy-start | bytes 9437188
  6.5 156.6 %reduce-scatter.5.cloned.1.call-start = ((), (), s32[]{:S(2)}) async-start(), calls=%async_computation.4 | async-start | bytes 589824 | tf_op jit(solution)/shard_map/reduce_scatter | solution.py:65
  38.1 20.1 %collective-permute-start = (f32[1024,128]{1,0:T(8,128)}, f32[1024,128]{1,0:T(8,128)}, u32[]{:S(2)}, u32[]{:S(2)}) collective-permute-start(f32[1024,128]{1,0:T(8,128)} %all_gather.12), channel_id=1, source_target_pairs={{8,0},{16,8},{24,16},{32,24},{40,32},{48,40},{56,48},{64,56},{72,6... | collective-permute-start | bytes 1572872 | tf_op jit(solution)/shard_map/ppermute | solution.py:14
  50.2 3.6 copy-start.3
  57.7 11.4 %collective-permute-start.3 = (f32[1024,128]{1,0:T(8,128)}, f32[1024,128]{1,0:T(8,128)}, u32[]{:S(2)}, u32[]{:S(2)}) collective-permute-start(f32[1024,128]{1,0:T(8,128)} %bitcast.14), channel_id=1, source_target_pairs={{248,0},{0,8},{8,16},{16,24},{24,32},{32,40},{40,48},{48,56},{56,6... | collective-permute-start | bytes 1572872 | tf_op jit(solution)/shard_map/ppermute | solution.py:14
  60.2 24.3 %collective-permute-start.1 = (f32[1024,128]{1,0:T(8,128)}, f32[1024,128]{1,0:T(8,128)}, u32[]{:S(2)}, u32[]{:S(2)}) collective-permute-start(f32[1024,128]{1,0:T(8,128)} %broadcast_select_fusion.7), channel_id=1, source_target_pairs={{16,0},{24,8},{32,16},{40,24},{48,32},{56,40},{64,48},{72,56},{80,... | collective-permute-start | bytes 1572872 | tf_op jit(solution)/shard_map/ppermute | solution.py:14
  71.1 26.0 %collective-permute-start.4 = (f32[1024,128]{1,0:T(8,128)}, f32[1024,128]{1,0:T(8,128)}, u32[]{:S(2)}, u32[]{:S(2)}) collective-permute-start(f32[1024,128]{1,0:T(8,128)} %broadcast_select_fusion.6), channel_id=1, source_target_pairs={{240,0},{248,8},{0,16},{8,24},{16,32},{24,40},{32,48},{40,56},{48,... | collective-permute-start | bytes 1572872 | tf_op jit(solution)/shard_map/ppermute | solution.py:14
  86.4 14.7 %collective-permute-start.2 = (f32[1024,128]{1,0:T(8,128)}, f32[1024,128]{1,0:T(8,128)}, u32[]{:S(2)}, u32[]{:S(2)}) collective-permute-start(f32[1024,128]{1,0:T(8,128)} %broadcast_select_fusion.15), channel_id=1, source_target_pairs={{32,0},{40,8},{48,16},{56,24},{64,32},{72,40},{80,48},{88,56},{96,... | collective-permute-start | bytes 1572872 | tf_op jit(solution)/shard_map/ppermute | solution.py:14
  99.0 22.1 %collective-permute-start.5 = (f32[1024,128]{1,0:T(8,128)}, f32[1024,128]{1,0:T(8,128)}, u32[]{:S(2)}, u32[]{:S(2)}) collective-permute-start(f32[1024,128]{1,0:T(8,128)} %broadcast_select_fusion.14), channel_id=1, source_target_pairs={{224,0},{232,8},{240,16},{248,24},{0,32},{8,40},{16,48},{24,56},{3... | collective-permute-start | bytes 1572872 | tf_op jit(solution)/shard_map/ppermute | solution.py:14
  123.1 186.2 %reduce-scatter.7.cloned.1.call-start = ((), (), s32[]{:S(2)}) async-start(), calls=%async_computation.5 | async-start | bytes 589824 | tf_op jit(solution)/shard_map/reduce_scatter | solution.py:65
  195.1 18.6 %collective-permute-start.6 = (f32[1024,128]{1,0:T(8,128)}, f32[1024,128]{1,0:T(8,128)}, u32[]{:S(2)}, u32[]{:S(2)}) collective-permute-start(f32[1024,128]{1,0:T(8,128)} %all_gather.13), channel_id=1, source_target_pairs={{8,0},{16,8},{24,16},{32,24},{40,32},{48,40},{56,48},{64,56},{72,6... | collective-permute-start | bytes 1572872 | tf_op jit(solution)/shard_map/ppermute | solution.py:14
  213.1 11.2 %collective-permute-start.9 = (f32[1024,128]{1,0:T(8,128)S(1)}, f32[1024,128]{1,0:T(8,128)S(1)}, u32[]{:S(2)}, u32[]{:S(2)}) collective-permute-start(f32[1024,128]{1,0:T(8,128)S(1)} %bitcast.102), channel_id=1, source_target_pairs={{248,0},{0,8},{8,16},{16,24},{24,32},{32,40},{40,48},{48,56},{56,6... | collective-permute-start | bytes 1572872 | tf_op jit(solution)/shard_map/ppermute | solution.py:14
  214.8 22.5 %collective-permute-start.7 = (f32[1024,128]{1,0:T(8,128)S(1)}, f32[1024,128]{1,0:T(8,128)S(1)}, u32[]{:S(2)}, u32[]{:S(2)}) collective-permute-start(f32[1024,128]{1,0:T(8,128)S(1)} %broadcast_select_fusion.5), channel_id=1, source_target_pairs={{16,0},{24,8},{32,16},{40,24},{48,32},{56,40},{64,48},{72,56},{80,... | collective-permute-start | bytes 1572872 | tf_op jit(solution)/shard_map/ppermute | solution.py:14
  224.4 25.3 %collective-permute-start.10 = (f32[1024,128]{1,0:T(8,128)S(1)}, f32[1024,128]{1,0:T(8,128)S(1)}, u32[]{:S(2)}, u32[]{:S(2)}) collective-permute-start(f32[1024,128]{1,0:T(8,128)S(1)} %broadcast_select_fusion.4), channel_id=1, source_target_pairs={{240,0},{248,8},{0,16},{8,24},{16,32},{24,40},{32,48},{40,56},{48,... | collective-permute-start | bytes 1572872 | tf_op jit(solution)/shard_map/ppermute | solution.py:14
  237.3 14.8 %collective-permute-start.8 = (f32[1024,128]{1,0:T(8,128)S(1)}, f32[1024,128]{1,0:T(8,128)S(1)}, u32[]{:S(2)}, u32[]{:S(2)}) collective-permute-start(f32[1024,128]{1,0:T(8,128)S(1)} %broadcast_select_fusion.13), channel_id=1, source_target_pairs={{32,0},{40,8},{48,16},{56,24},{64,32},{72,40},{80,48},{88,56},{96,... | collective-permute-start | bytes 1572872 | tf_op jit(solution)/shard_map/ppermute | solution.py:14
  250.5 20.6 %collective-permute-start.11 = (f32[1024,128]{1,0:T(8,128)}, f32[1024,128]{1,0:T(8,128)}, u32[]{:S(2)}, u32[]{:S(2)}) collective-permute-start(f32[1024,128]{1,0:T(8,128)} %broadcast_select_fusion.12), channel_id=1, source_target_pairs={{224,0},{232,8},{240,16},{248,24},{0,32},{8,40},{16,48},{24,56},{3... | collective-permute-start | bytes 1572872 | tf_op jit(solution)/shard_map/ppermute | solution.py:14
  267.9 41.5 %copy-start.1 = (f32[128,128]{1,0:T(8,128)S(1)}, f32[128,128]{1,0:T(8,128)}, u32[]{:S(2)}) copy-start(f32[128,128]{1,0:T(8,128)} %param.3) | copy-start | bytes 196612
  273.0 183.0 %reduce-scatter.9.cloned.1.call-start = ((), (), s32[]{:S(2)}) async-start(), calls=%async_computation.6 | async-start | bytes 589824 | tf_op jit(solution)/shard_map/reduce_scatter | solution.py:65
  341.3 18.8 %collective-permute-start.12 = (f32[1024,128]{1,0:T(8,128)}, f32[1024,128]{1,0:T(8,128)}, u32[]{:S(2)}, u32[]{:S(2)}) collective-permute-start(f32[1024,128]{1,0:T(8,128)} %all_gather.14), channel_id=1, source_target_pairs={{8,0},{16,8},{24,16},{32,24},{40,32},{48,40},{56,48},{64,56},{72,6... | collective-permute-start | bytes 1572872 | tf_op jit(solution)/shard_map/ppermute | solution.py:14
  359.5 11.2 %collective-permute-start.15 = (f32[1024,128]{1,0:T(8,128)S(1)}, f32[1024,128]{1,0:T(8,128)S(1)}, u32[]{:S(2)}, u32[]{:S(2)}) collective-permute-start(f32[1024,128]{1,0:T(8,128)S(1)} %bitcast.103), channel_id=1, source_target_pairs={{248,0},{0,8},{8,16},{16,24},{24,32},{32,40},{40,48},{48,56},{56,6... | collective-permute-start | bytes 1572872 | tf_op jit(solution)/shard_map/ppermute | solution.py:14
  361.2 22.5 %collective-permute-start.13 = (f32[1024,128]{1,0:T(8,128)S(1)}, f32[1024,128]{1,0:T(8,128)S(1)}, u32[]{:S(2)}, u32[]{:S(2)}) collective-permute-start(f32[1024,128]{1,0:T(8,128)S(1)} %broadcast_select_fusion.3), channel_id=1, source_target_pairs={{16,0},{24,8},{32,16},{40,24},{48,32},{56,40},{64,48},{72,56},{80,... | collective-permute-start | bytes 1572872 | tf_op jit(solution)/shard_map/ppermute | solution.py:14
  370.8 25.3 %collective-permute-start.16 = (f32[1024,128]{1,0:T(8,128)S(1)}, f32[1024,128]{1,0:T(8,128)S(1)}, u32[]{:S(2)}, u32[]{:S(2)}) collective-permute-start(f32[1024,128]{1,0:T(8,128)S(1)} %broadcast_select_fusion.2), channel_id=1, source_target_pairs={{240,0},{248,8},{0,16},{8,24},{16,32},{24,40},{32,48},{40,56},{48,... | collective-permute-start | bytes 1572872 | tf_op jit(solution)/shard_map/ppermute | solution.py:14
  383.7 15.1 %collective-permute-start.14 = (f32[1024,128]{1,0:T(8,128)S(1)}, f32[1024,128]{1,0:T(8,128)S(1)}, u32[]{:S(2)}, u32[]{:S(2)}) collective-permute-start(f32[1024,128]{1,0:T(8,128)S(1)} %broadcast_select_fusion.11), channel_id=1, source_target_pairs={{32,0},{40,8},{48,16},{56,24},{64,32},{72,40},{80,48},{88,56},{96,... | collective-permute-start | bytes 1572872 | tf_op jit(solution)/shard_map/ppermute | solution.py:14
  396.9 20.9 %collective-permute-start.17 = (f32[1024,128]{1,0:T(8,128)}, f32[1024,128]{1,0:T(8,128)}, u32[]{:S(2)}, u32[]{:S(2)}) collective-permute-start(f32[1024,128]{1,0:T(8,128)} %broadcast_select_fusion.10), channel_id=1, source_target_pairs={{224,0},{232,8},{240,16},{248,24},{0,32},{8,40},{16,48},{24,56},{3... | collective-permute-start | bytes 1572872 | tf_op jit(solution)/shard_map/ppermute | solution.py:14
  414.6 41.4 %copy-start.2 = (f32[128,128]{1,0:T(8,128)S(1)}, f32[128,128]{1,0:T(8,128)}, u32[]{:S(2)}) copy-start(f32[128,128]{1,0:T(8,128)} %reduce-scatter.5.cloned.1.call-done) | copy-start | bytes 196612
  419.8 182.5 %reduce-scatter.11.cloned.1.call-start = ((), (), s32[]{:S(2)}) async-start(), calls=%async_computation.7 | async-start | bytes 589824 | tf_op jit(solution)/shard_map/reduce_scatter | solution.py:65
  488.2 18.6 %collective-permute-start.18 = (f32[1024,128]{1,0:T(8,128)}, f32[1024,128]{1,0:T(8,128)}, u32[]{:S(2)}, u32[]{:S(2)}) collective-permute-start(f32[1024,128]{1,0:T(8,128)} %all_gather.15), channel_id=1, source_target_pairs={{8,0},{16,8},{24,16},{32,24},{40,32},{48,40},{56,48},{64,56},{72,6... | collective-permute-start | bytes 1572872 | tf_op jit(solution)/shard_map/ppermute | solution.py:14
  506.3 11.2 %collective-permute-start.21 = (f32[1024,128]{1,0:T(8,128)S(1)}, f32[1024,128]{1,0:T(8,128)S(1)}, u32[]{:S(2)}, u32[]{:S(2)}) collective-permute-start(f32[1024,128]{1,0:T(8,128)S(1)} %bitcast.101), channel_id=1, source_target_pairs={{248,0},{0,8},{8,16},{16,24},{24,32},{32,40},{40,48},{48,56},{56,6... | collective-permute-start | bytes 1572872 | tf_op jit(solution)/shard_map/ppermute | solution.py:14
  507.9 22.2 %collective-permute-start.19 = (f32[1024,128]{1,0:T(8,128)S(1)}, f32[1024,128]{1,0:T(8,128)S(1)}, u32[]{:S(2)}, u32[]{:S(2)}) collective-permute-start(f32[1024,128]{1,0:T(8,128)S(1)} %broadcast_select_fusion.1), channel_id=1, source_target_pairs={{16,0},{24,8},{32,16},{40,24},{48,32},{56,40},{64,48},{72,56},{80,... | collective-permute-start | bytes 1572872 | tf_op jit(solution)/shard_map/ppermute | solution.py:14
  517.5 25.0 %collective-permute-start.22 = (f32[1024,128]{1,0:T(8,128)S(1)}, f32[1024,128]{1,0:T(8,128)S(1)}, u32[]{:S(2)}, u32[]{:S(2)}) collective-permute-start(f32[1024,128]{1,0:T(8,128)S(1)} %broadcast_select_fusion), channel_id=1, source_target_pairs={{240,0},{248,8},{0,16},{8,24},{16,32},{24,40},{32,48},{40,56},{48,... | collective-permute-start | bytes 1572872 | tf_op jit(solution)/shard_map/ppermute | solution.py:14
  530.2 14.7 %collective-permute-start.20 = (f32[1024,128]{1,0:T(8,128)S(1)}, f32[1024,128]{1,0:T(8,128)S(1)}, u32[]{:S(2)}, u32[]{:S(2)}) collective-permute-start(f32[1024,128]{1,0:T(8,128)S(1)} %broadcast_select_fusion.9), channel_id=1, source_target_pairs={{32,0},{40,8},{48,16},{56,24},{64,32},{72,40},{80,48},{88,56},{96,... | collective-permute-start | bytes 1572872 | tf_op jit(solution)/shard_map/ppermute | solution.py:14
  543.4 20.4 %collective-permute-start.23 = (f32[1024,128]{1,0:T(8,128)}, f32[1024,128]{1,0:T(8,128)}, u32[]{:S(2)}, u32[]{:S(2)}) collective-permute-start(f32[1024,128]{1,0:T(8,128)} %broadcast_select_fusion.8), channel_id=1, source_target_pairs={{224,0},{232,8},{240,16},{248,24},{0,32},{8,40},{16,48},{24,56},{3... | collective-permute-start | bytes 1572872 | tf_op jit(solution)/shard_map/ppermute | solution.py:14
Sparse Core Ops, SparseCore 0:
  123.3 39.8 reduce-scatter.4
  273.2 36.1 reduce-scatter.6
  419.9 36.1 reduce-scatter.8
  566.0 36.2 reduce-scatter.10
where the time goes:
time: 619 us; the launch traced here: 611 us
  waiting for transfers between devices  222 us (36%)
  blocking collectives  125 us (20%)
  matrix products  87.2 us (14%)
  starting transfers between devices  73.7 us (12%)
  local copies, waits for them, and re-layouts  57.9 us (9%)
  other arithmetic  31.1 us (5%)
  between operations  13.7 us (2%)
    reduce_scatter x4, waiting for transfers between devices, fold(): return lax.psum_scatter(terms, 'off', scatter_dimension=0, tiled=True)  149 us
    all_gather x4, blocking collectives, spread(): return lax.all_gather(piece, 'off', axis=0, tiled=True)  125 us
    ppermute x24, starting transfers between devices, passed_along(): return lax.ppermute(block, axis, route)  73.5 us
    ppermute x24, waiting for transfers between devices, passed_along(): return lax.ppermute(block, axis, route)  73.1 us
    dot_general x4, matrix products, apply_tiles(): jnp.einsum('kab,kav->kbv', stored, own[row_list], precision=lax.Precision...  31.5 us
    dot_general x4, matrix products, apply_tiles(): jnp.einsum('kab,kbv->kav', stored, far_field[col_list], precision=lax.Pre...  31.5 us
    dot_general x4, local copies, waits for them, and re-layouts, apply_tiles(): jnp.einsum('kab,kbv->kav', stored, far_field[col_list], precision=lax.Pre...  14.3 us
    dot_general x4, local copies, waits for them, and re-layouts, apply_tiles(): jnp.einsum('kab,kav->kbv', stored, own[row_list], precision=lax.Precision...  14.3 us
  transfers between devices with their start and end apart: 28, of which 12 were waited for; matrix products, arithmetic and copies ran while one was open for 27% of the time, Pallas kernels for 0%

commit v1 on v0

--- a/solution.py
+++ b/solution.py
@@ -59,7 +59,9 @@
         return ahead.reshape(tile_rows, width) + returned
 
     def spread(piece):
-        return lax.all_gather(piece, "off", axis=0, tiled=True)
+        return jnp.concatenate(
+            lax.all_to_all(jnp.stack([piece] * lax.axis_size("off")), "off", 0, 0), axis=0
+        )
 
     def fold(terms):
         return lax.psum_scatter(terms, "off", scatter_dimension=0, tiled=True)

time: 619 us -> 547 us (0.88)
  blocking collectives: 125 us -> 34.3 us
  waiting for transfers between devices: 222 us -> 233 us
    all_gather x4 -> x0, blocking collectives: 125 us -> none  [spread(): return lax.all_gather(piece, 'off', axis=0, tiled=True)]
    all_to_all x0 -> x3, blocking collectives: none -> 34.3 us  [spread(): lax.all_to_all(jnp.stack([piece] * lax.axis_size('off')), 'off', 0, 0)]
    all_to_all x0 -> x1, waiting for transfers between devices: none -> 7.99 us  [spread(): lax.all_to_all(jnp.stack([piece] * lax.axis_size('off')), 'off', 0, 0)]
  transfers between devices with their start and end apart: 28 -> 29, of which waited for: 12 -> 13; matrix products, arithmetic and copies ran while one was open for 27% -> 31% of each run, Pallas kernels for 0% -> 0%
where the time goes in v1:
time: 547 us; the launch traced here: 538 us
  waiting for transfers between devices  233 us (43%)
  matrix products  87.5 us (16%)
  starting transfers between devices  78.6 us (14%)
  local copies, waits for them, and re-layouts  60.7 us (11%)
  blocking collectives  34.3 us (6%)
  other arithmetic  30.9 us (6%)
  between operations  13.8 us (3%)
    reduce_scatter x4, waiting for transfers between devices, fold(): return lax.psum_scatter(terms, 'off', scatter_dimension=0, tiled=True)  151 us
    ppermute x24, waiting for transfers between devices, passed_along(): return lax.ppermute(block, axis, route)  73.5 us
    ppermute x24, starting transfers between devices, passed_along(): return lax.ppermute(block, axis, route)  73.1 us
    all_to_all x3, blocking collectives, spread(): lax.all_to_all(jnp.stack([piece] * lax.axis_size('off')), 'off', 0, 0)  34.3 us
    dot_general x4, matrix products, apply_tiles(): jnp.einsum('kab,kbv->kav', stored, far_field[col_list], precision=lax.Pre...  31.7 us
    dot_general x4, matrix products, apply_tiles(): jnp.einsum('kab,kav->kbv', stored, own[row_list], precision=lax.Precision...  31.5 us
    dot_general x4, local copies, waits for them, and re-layouts, apply_tiles(): jnp.einsum('kab,kav->kbv', stored, own[row_list], precision=lax.Precision...  14.4 us
    dot_general x4, local copies, waits for them, and re-layouts, apply_tiles(): jnp.einsum('kab,kbv->kav', stored, far_field[col_list], precision=lax.Pre...  14.3 us
  transfers between devices with their start and end apart: 29, of which 13 were waited for; matrix products, arithmetic and copies ran while one was open for 31% of the time, Pallas kernels for 0%

profile of v1, /device:TPU:32, one launch (start us, length us, event | category | flops | bytes accessed | tf_op | source)
XLA Modules:
  0.0 538.2 jit_solution(873811269976412089)
XLA Ops:
  8.4 5.3 all-to-all-start
  15.3 8.0 %all-to-all-done = f32[8,128,128]{2,1,0:T(8,128)} async-done(((f32[8,128,128]{2,1,0:T(8,128)}), f32[8,128,128]{2,1,0:T(8,128)}, u32[]{:S(2)}, u32[]{:S(2)}) %all-to-all-start) | async-done | bytes 524320 | tf_op jit(solution)/shard_map/all_to_all | solution.py:63
  24.1 3.5 gather_fusion.1
  27.6 7.9 %fusion.28 = f32[48,128,128]{2,1,0:T(8,128)} fusion(f32[48,128,128]{2,1,0:T(8,128)} %gather_fusion.1, f32[1,1,48,128,128]{4,3,2,1,0:T(8,128)S(1)} %copy-done), kind=kOutput, calls=%fused_computation.36 | convolution fusion | flops 1207959552 | bytes 9437184 | tf_op jit(solution)/shard_map/kab,kav->kbv/dot_general | solution.py:47
  35.5 3.6 copy.13
  47.0 7.4 %collective-permute-done.3 = f32[1024,128]{1,0:T(8,128)} collective-permute-done((f32[1024,128]{1,0:T(8,128)}, f32[1024,128]{1,0:T(8,128)}, u32[]{:S(2)}, u32[]{:S(2)}) %collective-permute-start.3) | collective-permute-done | bytes 524320 | tf_op jit(solution)/shard_map/ppermute | solution.py:14
  56.3 12.3 %collective-permute-start.4 = (f32[1024,128]{1,0:T(8,128)}, f32[1024,128]{1,0:T(8,128)}, u32[]{:S(2)}, u32[]{:S(2)}) collective-permute-start(f32[1024,128]{1,0:T(8,128)} %broadcast_select_fusion.6), channel_id=1, source_target_pairs={{240,0},{248,8},{0,16},{8,24},{16,32},{24,40},{32,48},{40,56},{48,... | collective-permute-start | bytes 1572872 | tf_op jit(solution)/shard_map/ppermute | solution.py:14
  70.7 10.6 %collective-permute-done.4 = f32[1024,128]{1,0:T(8,128)} collective-permute-done((f32[1024,128]{1,0:T(8,128)}, f32[1024,128]{1,0:T(8,128)}, u32[]{:S(2)}, u32[]{:S(2)}) %collective-permute-start.4) | collective-permute-done | bytes 524320 | tf_op jit(solution)/shard_map/ppermute | solution.py:14
  87.1 3.4 gather_fusion
  90.6 7.9 %fusion.30 = f32[48,128,128]{2,1,0:T(8,128)} fusion(f32[48,128,128]{2,1,0:T(8,128)} %gather_fusion, f32[1,1,48,128,128]{4,3,2,1,0:T(8,128)S(1)} %copy-done), kind=kOutput, calls=%fused_computation.38 | convolution fusion | flops 1207959552 | bytes 9437184 | tf_op jit(solution)/shard_map/kab,kbv->kav/dot_general | solution.py:55
  98.5 3.6 copy.12
  107.2 38.9 %reduce-scatter.5.cloned.1.call-done = f32[128,128]{1,0:T(8,128)} async-done(((f32[1024,128]{1,0:T(8,128)}), f32[128,128]{1,0:T(8,128)}) %reduce-scatter.5.cloned.1.call-update) | async-done | bytes 65552 | tf_op jit(solution)/shard_map/reduce_scatter | solution.py:67
  147.0 11.4 %all_to_all.20 = f32[8,128,128]{2,1,0:T(8,128)} all-to-all(f32[8,128,128]{2,1,0:T(8,128)S(1)} %stack.9), channel_id=1, replica_groups=mesh['row'=32,'off'=8] {'off'}, dimensions={0} | all-to-all | bytes 1048576 | tf_op jit(solution)/shard_map/all_to_all | solution.py:63
  158.4 3.5 gather_fusion.3
  162.0 7.9 %fusion.24 = f32[48,128,128]{2,1,0:T(8,128)} fusion(f32[48,128,128]{2,1,0:T(8,128)} %gather_fusion.3, f32[1,1,48,128,128]{4,3,2,1,0:T(8,128)S(1)} %copy-done), kind=kOutput, calls=%fused_computation.32 | convolution fusion | flops 1207959552 | bytes 9437184 | tf_op jit(solution)/shard_map/kab,kav->kbv/dot_general | solution.py:47
  169.8 3.6 copy.15
  178.2 3.2 collective-permute-start.7
  181.4 6.4 %collective-permute-done.9 = f32[1024,128]{1,0:T(8,128)S(1)} collective-permute-done((f32[1024,128]{1,0:T(8,128)S(1)}, f32[1024,128]{1,0:T(8,128)S(1)}, u32[]{:S(2)}, u32[]{:S(2)}) %collective-permute-start.9) | collective-permute-done | bytes 524320 | tf_op jit(solution)/shard_map/ppermute | solution.py:14
  187.8 13.0 %collective-permute-start.10 = (f32[1024,128]{1,0:T(8,128)S(1)}, f32[1024,128]{1,0:T(8,128)S(1)}, u32[]{:S(2)}, u32[]{:S(2)}) collective-permute-start(f32[1024,128]{1,0:T(8,128)S(1)} %broadcast_select_fusion.4), channel_id=1, source_target_pairs={{240,0},{248,8},{0,16},{8,24},{16,32},{24,40},{32,48},{40,56},{48,... | collective-permute-start | bytes 1572872 | tf_op jit(solution)/shard_map/ppermute | solution.py:14
  201.5 11.7 %collective-permute-done.10 = f32[1024,128]{1,0:T(8,128)S(1)} collective-permute-done((f32[1024,128]{1,0:T(8,128)S(1)}, f32[1024,128]{1,0:T(8,128)S(1)}, u32[]{:S(2)}, u32[]{:S(2)}) %collective-permute-start.10) | collective-permute-done | bytes 524320 | tf_op jit(solution)/shard_map/ppermute | solution.py:14
  216.5 3.4 gather_fusion.2
  219.9 7.9 %fusion.26 = f32[48,128,128]{2,1,0:T(8,128)} fusion(f32[48,128,128]{2,1,0:T(8,128)} %gather_fusion.2, f32[1,1,48,128,128]{4,3,2,1,0:T(8,128)S(1)} %copy-done), kind=kOutput, calls=%fused_computation.34 | convolution fusion | flops 1207959552 | bytes 9437184 | tf_op jit(solution)/shard_map/kab,kbv->kav/dot_general | solution.py:55
  227.8 3.6 copy.14
  231.4 3.0 fusion.10
  236.6 37.2 %reduce-scatter.7.cloned.1.call-done = f32[128,128]{1,0:T(8,128)} async-done(((f32[1024,128]{1,0:T(8,128)}), f32[128,128]{1,0:T(8,128)}) %reduce-scatter.7.cloned.1.call-update) | async-done | bytes 65552 | tf_op jit(solution)/shard_map/reduce_scatter | solution.py:67
  274.7 11.4 %all_to_all.21 = f32[8,128,128]{2,1,0:T(8,128)} all-to-all(f32[8,128,128]{2,1,0:T(8,128)S(1)} %stack.10), channel_id=1, replica_groups=mesh['row'=32,'off'=8] {'off'}, dimensions={0} | all-to-all | bytes 1048576 | tf_op jit(solution)/shard_map/all_to_all | solution.py:63
  286.3 3.5 gather_fusion.5
  289.8 7.9 %fusion.20 = f32[48,128,128]{2,1,0:T(8,128)} fusion(f32[48,128,128]{2,1,0:T(8,128)} %gather_fusion.5, f32[1,1,48,128,128]{4,3,2,1,0:T(8,128)S(1)} %copy-done), kind=kOutput, calls=%fused_computation.28 | convolution fusion | flops 1207959552 | bytes 9437184 | tf_op jit(solution)/shard_map/kab,kav->kbv/dot_general | solution.py:47
  297.7 3.6 copy.17
  308.7 6.9 %collective-permute-done.15 = f32[1024,128]{1,0:T(8,128)S(1)} collective-permute-done((f32[1024,128]{1,0:T(8,128)S(1)}, f32[1024,128]{1,0:T(8,128)S(1)}, u32[]{:S(2)}, u32[]{:S(2)}) %collective-permute-start.15) | collective-permute-done | bytes 524320 | tf_op jit(solution)/shard_map/ppermute | solution.py:14
  315.7 13.1 %collective-permute-start.16 = (f32[1024,128]{1,0:T(8,128)S(1)}, f32[1024,128]{1,0:T(8,128)S(1)}, u32[]{:S(2)}, u32[]{:S(2)}) collective-permute-start(f32[1024,128]{1,0:T(8,128)S(1)} %broadcast_select_fusion.2), channel_id=1, source_target_pairs={{240,0},{248,8},{0,16},{8,24},{16,32},{24,40},{32,48},{40,56},{48,... | collective-permute-start | bytes 1572872 | tf_op jit(solution)/shard_map/ppermute | solution.py:14
  329.2 11.9 %collective-permute-done.16 = f32[1024,128]{1,0:T(8,128)S(1)} collective-permute-done((f32[1024,128]{1,0:T(8,128)S(1)}, f32[1024,128]{1,0:T(8,128)S(1)}, u32[]{:S(2)}, u32[]{:S(2)}) %collective-permute-start.16) | collective-permute-done | bytes 524320 | tf_op jit(solution)/shard_map/ppermute | solution.py:14
  344.4 3.4 gather_fusion.4
  347.8 7.9 %fusion.22 = f32[48,128,128]{2,1,0:T(8,128)} fusion(f32[48,128,128]{2,1,0:T(8,128)} %gather_fusion.4, f32[1,1,48,128,128]{4,3,2,1,0:T(8,128)S(1)} %copy-done), kind=kOutput, calls=%fused_computation.30 | convolution fusion | flops 1207959552 | bytes 9437184 | tf_op jit(solution)/shard_map/kab,kbv->kav/dot_general | solution.py:55
  355.8 3.6 copy.16
  359.4 3.0 fusion.6
  364.5 37.5 %reduce-scatter.9.cloned.1.call-done = f32[128,128]{1,0:T(8,128)} async-done(((f32[1024,128]{1,0:T(8,128)}), f32[128,128]{1,0:T(8,128)}) %reduce-scatter.9.cloned.1.call-update) | async-done | bytes 65552 | tf_op jit(solution)/shard_map/reduce_scatter | solution.py:67
  403.0 11.4 %all_to_all.22 = f32[8,128,128]{2,1,0:T(8,128)} all-to-all(f32[8,128,128]{2,1,0:T(8,128)S(1)} %stack.11), channel_id=1, replica_groups=mesh['row'=32,'off'=8] {'off'}, dimensions={0} | all-to-all | bytes 1048576 | tf_op jit(solution)/shard_map/all_to_all | solution.py:63
  414.4 3.5 gather_fusion.7
  417.9 7.9 %fusion.16 = f32[48,128,128]{2,1,0:T(8,128)} fusion(f32[48,128,128]{2,1,0:T(8,128)} %gather_fusion.7, f32[1,1,48,128,128]{4,3,2,1,0:T(8,128)S(1)} %copy-done), kind=kOutput, calls=%fused_computation.24 | convolution fusion | flops 1207959552 | bytes 9437184 | tf_op jit(solution)/shard_map/kab,kav->kbv/dot_general | solution.py:47
  425.8 3.6 copy.19
  437.0 6.7 %collective-permute-done.21 = f32[1024,128]{1,0:T(8,128)S(1)} collective-permute-done((f32[1024,128]{1,0:T(8,128)S(1)}, f32[1024,128]{1,0:T(8,128)S(1)}, u32[]{:S(2)}, u32[]{:S(2)}) %collective-permute-start.21) | collective-permute-done | bytes 524320 | tf_op jit(solution)/shard_map/ppermute | solution.py:14
  443.8 13.0 %collective-permute-start.22 = (f32[1024,128]{1,0:T(8,128)S(1)}, f32[1024,128]{1,0:T(8,128)S(1)}, u32[]{:S(2)}, u32[]{:S(2)}) collective-permute-start(f32[1024,128]{1,0:T(8,128)S(1)} %broadcast_select_fusion), channel_id=1, source_target_pairs={{240,0},{248,8},{0,16},{8,24},{16,32},{24,40},{32,48},{40,56},{48,... | collective-permute-start | bytes 1572872 | tf_op jit(solution)/shard_map/ppermute | solution.py:14
  457.3 11.8 %collective-permute-done.22 = f32[1024,128]{1,0:T(8,128)S(1)} collective-permute-done((f32[1024,128]{1,0:T(8,128)S(1)}, f32[1024,128]{1,0:T(8,128)S(1)}, u32[]{:S(2)}, u32[]{:S(2)}) %collective-permute-start.22) | collective-permute-done | bytes 524320 | tf_op jit(solution)/shard_map/ppermute | solution.py:14
  472.4 3.4 gather_fusion.6
  475.8 7.9 %fusion.18 = f32[48,128,128]{2,1,0:T(8,128)} fusion(f32[48,128,128]{2,1,0:T(8,128)} %gather_fusion.6, f32[1,1,48,128,128]{4,3,2,1,0:T(8,128)S(1)} %copy-done), kind=kOutput, calls=%fused_computation.26 | convolution fusion | flops 1207959552 | bytes 9437184 | tf_op jit(solution)/shard_map/kab,kbv->kav/dot_general | solution.py:55
  483.7 3.6 copy.18
  492.4 37.3 %reduce-scatter.11.cloned.1.call-done = f32[128,128]{1,0:T(8,128)} async-done(((f32[1024,128]{1,0:T(8,128)}), f32[128,128]{1,0:T(8,128)}) %reduce-scatter.11.cloned.1.call-update) | async-done | bytes 65552 | tf_op jit(solution)/shard_map/reduce_scatter | solution.py:67
  (99 shorter events, 72.1 us)
Async XLA Ops:
  6.5 21.1 %copy-start = (f32[1,1,48,128,128]{4,3,2,1,0:T(8,128)S(1)}, f32[1,1,48,128,128]{4,3,2,1,0:T(8,128)}, u32[]{:S(2)}) copy-start(f32[1,1,48,128,128]{4,3,2,1,0:T(8,128)} %param.4) | copy-start | bytes 9437188
  8.4 14.9 %all-to-all-start = ((f32[8,128,128]{2,1,0:T(8,128)}), f32[8,128,128]{2,1,0:T(8,128)}, u32[]{:S(2)}, u32[]{:S(2)}) async-start(f32[8,128,128]{2,1,0:T(8,128)} %stack.8), calls=%async_computation | async-start | bytes 1048576 | tf_op jit(solution)/shard_map/all_to_all | solution.py:63
  13.7 132.5 %reduce-scatter.5.cloned.1.call-start = ((), (), s32[]{:S(2)}) async-start(), calls=%async_computation.8 | async-start | bytes 589824 | tf_op jit(solution)/shard_map/reduce_scatter | solution.py:67
  23.3 19.8 %collective-permute-start = (f32[1024,128]{1,0:T(8,128)}, f32[1024,128]{1,0:T(8,128)}, u32[]{:S(2)}, u32[]{:S(2)}) collective-permute-start(f32[1024,128]{1,0:T(8,128)} %bitcast.2), channel_id=1, source_target_pairs={{8,0},{16,8},{24,16},{32,24},{40,32},{48,40},{56,48},{64,56},{72,6... | collective-permute-start | bytes 1572872 | tf_op jit(solution)/shard_map/ppermute | solution.py:14
  43.0 11.4 %collective-permute-start.3 = (f32[1024,128]{1,0:T(8,128)}, f32[1024,128]{1,0:T(8,128)}, u32[]{:S(2)}, u32[]{:S(2)}) collective-permute-start(f32[1024,128]{1,0:T(8,128)} %bitcast.14), channel_id=1, source_target_pairs={{248,0},{0,8},{8,16},{16,24},{24,32},{32,40},{40,48},{48,56},{56,6... | collective-permute-start | bytes 1572872 | tf_op jit(solution)/shard_map/ppermute | solution.py:14
  44.9 23.7 %collective-permute-start.1 = (f32[1024,128]{1,0:T(8,128)}, f32[1024,128]{1,0:T(8,128)}, u32[]{:S(2)}, u32[]{:S(2)}) collective-permute-start(f32[1024,128]{1,0:T(8,128)} %broadcast_select_fusion.7), channel_id=1, source_target_pairs={{16,0},{24,8},{32,16},{40,24},{48,32},{56,40},{64,48},{72,56},{80,... | collective-permute-start | bytes 1572872 | tf_op jit(solution)/shard_map/ppermute | solution.py:14
  56.3 24.9 %collective-permute-start.4 = (f32[1024,128]{1,0:T(8,128)}, f32[1024,128]{1,0:T(8,128)}, u32[]{:S(2)}, u32[]{:S(2)}) collective-permute-start(f32[1024,128]{1,0:T(8,128)} %broadcast_select_fusion.6), channel_id=1, source_target_pairs={{240,0},{248,8},{0,16},{8,24},{16,32},{24,40},{32,48},{40,56},{48,... | collective-permute-start | bytes 1572872 | tf_op jit(solution)/shard_map/ppermute | solution.py:14
  70.5 14.7 %collective-permute-start.2 = (f32[1024,128]{1,0:T(8,128)}, f32[1024,128]{1,0:T(8,128)}, u32[]{:S(2)}, u32[]{:S(2)}) collective-permute-start(f32[1024,128]{1,0:T(8,128)} %broadcast_select_fusion.15), channel_id=1, source_target_pairs={{32,0},{40,8},{48,16},{56,24},{64,32},{72,40},{80,48},{88,56},{96,... | collective-permute-start | bytes 1572872 | tf_op jit(solution)/shard_map/ppermute | solution.py:14
  83.1 22.1 %collective-permute-start.5 = (f32[1024,128]{1,0:T(8,128)}, f32[1024,128]{1,0:T(8,128)}, u32[]{:S(2)}, u32[]{:S(2)}) collective-permute-start(f32[1024,128]{1,0:T(8,128)} %broadcast_select_fusion.14), channel_id=1, source_target_pairs={{224,0},{232,8},{240,16},{248,24},{0,32},{8,40},{16,48},{24,56},{3... | collective-permute-start | bytes 1572872 | tf_op jit(solution)/shard_map/ppermute | solution.py:14
  107.2 166.6 %reduce-scatter.7.cloned.1.call-start = ((), (), s32[]{:S(2)}) async-start(), calls=%async_computation.9 | async-start | bytes 589824 | tf_op jit(solution)/shard_map/reduce_scatter | solution.py:67
  158.4 18.7 %collective-permute-start.6 = (f32[1024,128]{1,0:T(8,128)}, f32[1024,128]{1,0:T(8,128)}, u32[]{:S(2)}, u32[]{:S(2)}) collective-permute-start(f32[1024,128]{1,0:T(8,128)} %bitcast.15), channel_id=1, source_target_pairs={{8,0},{16,8},{24,16},{32,24},{40,32},{48,40},{56,48},{64,56},{72,6... | collective-permute-start | bytes 1572872 | tf_op jit(solution)/shard_map/ppermute | solution.py:14
  176.6 11.2 %collective-permute-start.9 = (f32[1024,128]{1,0:T(8,128)S(1)}, f32[1024,128]{1,0:T(8,128)S(1)}, u32[]{:S(2)}, u32[]{:S(2)}) collective-permute-start(f32[1024,128]{1,0:T(8,128)S(1)} %bitcast.106), channel_id=1, source_target_pairs={{248,0},{0,8},{8,16},{16,24},{24,32},{32,40},{40,48},{48,56},{56,6... | collective-permute-start | bytes 1572872 | tf_op jit(solution)/shard_map/ppermute | solution.py:14
  178.2 22.6 %collective-permute-start.7 = (f32[1024,128]{1,0:T(8,128)S(1)}, f32[1024,128]{1,0:T(8,128)S(1)}, u32[]{:S(2)}, u32[]{:S(2)}) collective-permute-start(f32[1024,128]{1,0:T(8,128)S(1)} %broadcast_select_fusion.5), channel_id=1, source_target_pairs={{16,0},{24,8},{32,16},{40,24},{48,32},{56,40},{64,48},{72,56},{80,... | collective-permute-start | bytes 1572872 | tf_op jit(solution)/shard_map/ppermute | solution.py:14
  187.8 25.4 %collective-permute-start.10 = (f32[1024,128]{1,0:T(8,128)S(1)}, f32[1024,128]{1,0:T(8,128)S(1)}, u32[]{:S(2)}, u32[]{:S(2)}) collective-permute-start(f32[1024,128]{1,0:T(8,128)S(1)} %broadcast_select_fusion.4), channel_id=1, source_target_pairs={{240,0},{248,8},{0,16},{8,24},{16,32},{24,40},{32,48},{40,56},{48,... | collective-permute-start | bytes 1572872 | tf_op jit(solution)/shard_map/ppermute | solution.py:14
  200.9 14.7 %collective-permute-start.8 = (f32[1024,128]{1,0:T(8,128)S(1)}, f32[1024,128]{1,0:T(8,128)S(1)}, u32[]{:S(2)}, u32[]{:S(2)}) collective-permute-start(f32[1024,128]{1,0:T(8,128)S(1)} %broadcast_select_fusion.13), channel_id=1, source_target_pairs={{32,0},{40,8},{48,16},{56,24},{64,32},{72,40},{80,48},{88,56},{96,... | collective-permute-start | bytes 1572872 | tf_op jit(solution)/shard_map/ppermute | solution.py:14
  214.0 20.5 %collective-permute-start.11 = (f32[1024,128]{1,0:T(8,128)}, f32[1024,128]{1,0:T(8,128)}, u32[]{:S(2)}, u32[]{:S(2)}) collective-permute-start(f32[1024,128]{1,0:T(8,128)} %broadcast_select_fusion.12), channel_id=1, source_target_pairs={{224,0},{232,8},{240,16},{248,24},{0,32},{8,40},{16,48},{24,56},{3... | collective-permute-start | bytes 1572872 | tf_op jit(solution)/shard_map/ppermute | solution.py:14
  231.4 42.4 %copy-start.1 = (f32[128,128]{1,0:T(8,128)S(1)}, f32[128,128]{1,0:T(8,128)}, u32[]{:S(2)}) copy-start(f32[128,128]{1,0:T(8,128)} %param.3) | copy-start | bytes 196612
  236.5 165.5 %reduce-scatter.9.cloned.1.call-start = ((), (), s32[]{:S(2)}) async-start(), calls=%async_computation.10 | async-start | bytes 589824 | tf_op jit(solution)/shard_map/reduce_scatter | solution.py:67
  286.1 18.8 %collective-permute-start.12 = (f32[1024,128]{1,0:T(8,128)}, f32[1024,128]{1,0:T(8,128)}, u32[]{:S(2)}, u32[]{:S(2)}) collective-permute-start(f32[1024,128]{1,0:T(8,128)} %bitcast.21), channel_id=1, source_target_pairs={{8,0},{16,8},{24,16},{32,24},{40,32},{48,40},{56,48},{64,56},{72,6... | collective-permute-start | bytes 1572872 | tf_op jit(solution)/shard_map/ppermute | solution.py:14
  304.4 11.2 %collective-permute-start.15 = (f32[1024,128]{1,0:T(8,128)S(1)}, f32[1024,128]{1,0:T(8,128)S(1)}, u32[]{:S(2)}, u32[]{:S(2)}) collective-permute-start(f32[1024,128]{1,0:T(8,128)S(1)} %bitcast.107), channel_id=1, source_target_pairs={{248,0},{0,8},{8,16},{16,24},{24,32},{32,40},{40,48},{48,56},{56,6... | collective-permute-start | bytes 1572872 | tf_op jit(solution)/shard_map/ppermute | solution.py:14
  306.1 22.7 %collective-permute-start.13 = (f32[1024,128]{1,0:T(8,128)S(1)}, f32[1024,128]{1,0:T(8,128)S(1)}, u32[]{:S(2)}, u32[]{:S(2)}) collective-permute-start(f32[1024,128]{1,0:T(8,128)S(1)} %broadcast_select_fusion.3), channel_id=1, source_target_pairs={{16,0},{24,8},{32,16},{40,24},{48,32},{56,40},{64,48},{72,56},{80,... | collective-permute-start | bytes 1572872 | tf_op jit(solution)/shard_map/ppermute | solution.py:14
  315.7 25.4 %collective-permute-start.16 = (f32[1024,128]{1,0:T(8,128)S(1)}, f32[1024,128]{1,0:T(8,128)S(1)}, u32[]{:S(2)}, u32[]{:S(2)}) collective-permute-start(f32[1024,128]{1,0:T(8,128)S(1)} %broadcast_select_fusion.2), channel_id=1, source_target_pairs={{240,0},{248,8},{0,16},{8,24},{16,32},{24,40},{32,48},{40,56},{48,... | collective-permute-start | bytes 1572872 | tf_op jit(solution)/shard_map/ppermute | solution.py:14
  328.8 14.7 %collective-permute-start.14 = (f32[1024,128]{1,0:T(8,128)S(1)}, f32[1024,128]{1,0:T(8,128)S(1)}, u32[]{:S(2)}, u32[]{:S(2)}) collective-permute-start(f32[1024,128]{1,0:T(8,128)S(1)} %broadcast_select_fusion.11), channel_id=1, source_target_pairs={{32,0},{40,8},{48,16},{56,24},{64,32},{72,40},{80,48},{88,56},{96,... | collective-permute-start | bytes 1572872 | tf_op jit(solution)/shard_map/ppermute | solution.py:14
  341.9 20.6 %collective-permute-start.17 = (f32[1024,128]{1,0:T(8,128)}, f32[1024,128]{1,0:T(8,128)}, u32[]{:S(2)}, u32[]{:S(2)}) collective-permute-start(f32[1024,128]{1,0:T(8,128)} %broadcast_select_fusion.10), channel_id=1, source_target_pairs={{224,0},{232,8},{240,16},{248,24},{0,32},{8,40},{16,48},{24,56},{3... | collective-permute-start | bytes 1572872 | tf_op jit(solution)/shard_map/ppermute | solution.py:14
  359.3 42.7 %copy-start.2 = (f32[128,128]{1,0:T(8,128)S(1)}, f32[128,128]{1,0:T(8,128)}, u32[]{:S(2)}) copy-start(f32[128,128]{1,0:T(8,128)} %reduce-scatter.5.cloned.1.call-done) | copy-start | bytes 196612
  364.5 165.2 %reduce-scatter.11.cloned.1.call-start = ((), (), s32[]{:S(2)}) async-start(), calls=%async_computation.11 | async-start | bytes 589824 | tf_op jit(solution)/shard_map/reduce_scatter | solution.py:67
  414.4 18.7 %collective-permute-start.18 = (f32[1024,128]{1,0:T(8,128)}, f32[1024,128]{1,0:T(8,128)}, u32[]{:S(2)}, u32[]{:S(2)}) collective-permute-start(f32[1024,128]{1,0:T(8,128)} %bitcast.27), channel_id=1, source_target_pairs={{8,0},{16,8},{24,16},{32,24},{40,32},{48,40},{56,48},{64,56},{72,6... | collective-permute-start | bytes 1572872 | tf_op jit(solution)/shard_map/ppermute | solution.py:14
  432.5 11.2 %collective-permute-start.21 = (f32[1024,128]{1,0:T(8,128)S(1)}, f32[1024,128]{1,0:T(8,128)S(1)}, u32[]{:S(2)}, u32[]{:S(2)}) collective-permute-start(f32[1024,128]{1,0:T(8,128)S(1)} %bitcast.105), channel_id=1, source_target_pairs={{248,0},{0,8},{8,16},{16,24},{24,32},{32,40},{40,48},{48,56},{56,6... | collective-permute-start | bytes 1572872 | tf_op jit(solution)/shard_map/ppermute | solution.py:14
  434.2 22.6 %collective-permute-start.19 = (f32[1024,128]{1,0:T(8,128)S(1)}, f32[1024,128]{1,0:T(8,128)S(1)}, u32[]{:S(2)}, u32[]{:S(2)}) collective-permute-start(f32[1024,128]{1,0:T(8,128)S(1)} %broadcast_select_fusion.1), channel_id=1, source_target_pairs={{16,0},{24,8},{32,16},{40,24},{48,32},{56,40},{64,48},{72,56},{80,... | collective-permute-start | bytes 1572872 | tf_op jit(solution)/shard_map/ppermute | solution.py:14
  443.8 25.3 %collective-permute-start.22 = (f32[1024,128]{1,0:T(8,128)S(1)}, f32[1024,128]{1,0:T(8,128)S(1)}, u32[]{:S(2)}, u32[]{:S(2)}) collective-permute-start(f32[1024,128]{1,0:T(8,128)S(1)} %broadcast_select_fusion), channel_id=1, source_target_pairs={{240,0},{248,8},{0,16},{8,24},{16,32},{24,40},{32,48},{40,56},{48,... | collective-permute-start | bytes 1572872 | tf_op jit(solution)/shard_map/ppermute | solution.py:14
  456.8 14.7 %collective-permute-start.20 = (f32[1024,128]{1,0:T(8,128)S(1)}, f32[1024,128]{1,0:T(8,128)S(1)}, u32[]{:S(2)}, u32[]{:S(2)}) collective-permute-start(f32[1024,128]{1,0:T(8,128)S(1)} %broadcast_select_fusion.9), channel_id=1, source_target_pairs={{32,0},{40,8},{48,16},{56,24},{64,32},{72,40},{80,48},{88,56},{96,... | collective-permute-start | bytes 1572872 | tf_op jit(solution)/shard_map/ppermute | solution.py:14
  469.9 20.5 %collective-permute-start.23 = (f32[1024,128]{1,0:T(8,128)}, f32[1024,128]{1,0:T(8,128)}, u32[]{:S(2)}, u32[]{:S(2)}) collective-permute-start(f32[1024,128]{1,0:T(8,128)} %broadcast_select_fusion.8), channel_id=1, source_target_pairs={{224,0},{232,8},{240,16},{248,24},{0,32},{8,40},{16,48},{24,56},{3... | collective-permute-start | bytes 1572872 | tf_op jit(solution)/shard_map/ppermute | solution.py:14
Sparse Core Ops, SparseCore 0:
  107.3 38.7 reduce-scatter.4
  236.7 37.1 reduce-scatter.6
  364.6 37.4 reduce-scatter.8
  492.5 37.1 reduce-scatter.10
